TPU v7x, 128 devices: a whole 4x4x4 slice. The times are simulated.
128 devices in a mesh: segment: 2 (over x_lo), seq: 16 (over z, y), mp: 4 (over x_hi, core).
Axes of the slice: x: 4 (x_hi: 2, x_lo: 2; x = x_hi * 2 + x_lo), y: 4, z: 4, core: 2. Of those that a mesh axis runs over, the one named last changes fastest.
Arguments:
- memory: bfloat16 [2, 4096, 4096], P(None, 'seq', 'mp')
- decoder_rows: bfloat16 [2, 1024, 4096], P(None, 'seq', 'mp')
- gains: bfloat16 [2, 4096], P('segment'), may hold values from 0.5 to 1.5
- weights: bfloat16 [2, 2, 4096, 4096], P('segment', None, None, 'mp')
- lengths: int32 [2], replicated, may hold values from 512 to 4096, as said below
Outputs:
- decoder_out: bfloat16 [2, 1024, 4096], P(None, 'seq', ('segment', 'mp'))
Inputs may be any that keep to these rules, and one draw needn't show every extreme that they name: memory positions of document b at or beyond lengths[b] are padding; some document has all 4096 positions.
All inputs are finite; a program needn't handle non-finite values.
Results may differ from a plain program's by a relative error of at most 0.015.
The roundings to bfloat16 on the way count: a program that leaves them out, or rounds other values in their place, can miss the bound.
Values may be sent and summed in bfloat16 or wider, within the bound.
A program may use at most 192 MiB of HBM per device.

v0:
```python
import jax
import jax.numpy as jnp
from jax import lax
from jax.sharding import PartitionSpec as P

DKV = 64
norm_eps = 1e-06
masked_score = -1e30


def passed_along(shard, axis, by):
    count = lax.axis_size(axis)
    pairs = [(i, i + by) for i in range(count) if 0 <= i + by < count]
    return lax.ppermute(shard, axis, pairs)


def rms_rows(rows, gain):
    wide = rows.astype(jnp.float32)
    inverse = lax.rsqrt(jnp.mean(wide * wide, axis=1, keepdims=True) + norm_eps)
    return (wide * inverse * gain.astype(jnp.float32)[None, :]).astype(jnp.bfloat16)


def fold_block(running, queries, key_block, value_block, first_pos, lengths):
    maxima, totals, summed = running
    doc_count, span = (key_block.shape[0], key_block.shape[1])
    heads_here = queries.shape[2]
    key_heads = key_block.reshape(doc_count, span, heads_here, DKV)
    value_heads = value_block.reshape(doc_count, span, heads_here, DKV)
    scores = jnp.einsum("bqhd,bkhd->bhqk", queries, key_heads, preferred_element_type=jnp.float32)
    positions = first_pos + lax.iota(jnp.int32, span)
    valid_keys = (positions[None, :] < lengths[:, None])[:, None, None, :]
    masked = jnp.where(valid_keys, scores, masked_score)
    new_max = jnp.maximum(maxima, jnp.max(masked, axis=-1))
    exp_scores = jnp.where(valid_keys, jnp.exp(masked - new_max[..., None]), 0.0)
    rescale = jnp.exp(maxima - new_max)
    totals = totals * rescale + jnp.sum(exp_scores, axis=-1)
    summed = summed * rescale[..., None] + jnp.einsum(
        "bhqk,bkhd->bhqd",
        exp_scores.astype(jnp.bfloat16),
        value_heads,
        preferred_element_type=jnp.float32,
    )
    return (new_max, totals, summed)


def on_device(memory, decoder_rows, gains, weights, lengths):
    segment_index = lax.axis_index("segment")
    decoding = segment_index == 1
    doc_count, mem_dev, part_width = memory.shape
    pos_dev = decoder_rows.shape[1]
    mem_count = doc_count * mem_dev
    row_count = doc_count * pos_dev
    mem_full, dec_full = (
        lax.all_gather(memory.reshape(mem_count, part_width), "mp", axis=1, tiled=True),
        lax.all_gather(decoder_rows.reshape(row_count, part_width), "mp", axis=1, tiled=True),
    )
    first_weight = weights[0, 0]
    second_weight = weights[0, 1]
    section_gain = gains[0]
    head_width = first_weight.shape[1]
    heads_here = head_width // DKV

    def encode(source):
        normed = rms_rows(source, section_gain)
        key_out = jnp.dot(normed, first_weight, preferred_element_type=jnp.float32).astype(
            jnp.bfloat16
        )
        value_out = jnp.dot(normed, second_weight, preferred_element_type=jnp.float32).astype(
            jnp.bfloat16
        )
        return (key_out, value_out)

    def skip_encode(source):
        empty = jnp.zeros((mem_count, head_width), jnp.bfloat16)
        return (empty, empty)

    key_local, value_local = lax.cond(decoding, skip_encode, encode, mem_full)
    query_rows = lax.cond(
        decoding,
        lambda source: jnp.dot(
            rms_rows(source, section_gain), first_weight, preferred_element_type=jnp.float32
        ).astype(jnp.bfloat16),
        lambda source: jnp.zeros((row_count, head_width), jnp.bfloat16),
        dec_full,
    )
    key_rows, value_rows = passed_along((key_local, value_local), "segment", 1)
    key_flat = key_rows.reshape(doc_count, mem_dev, head_width)
    value_flat = value_rows.reshape(doc_count, mem_dev, head_width)
    queries = query_rows.reshape(doc_count, pos_dev, heads_here, DKV)
    start_state = (
        jnp.full((doc_count, heads_here, pos_dev), masked_score, jnp.float32),
        jnp.zeros((doc_count, heads_here, pos_dev), jnp.float32),
        jnp.zeros((doc_count, heads_here, pos_dev, DKV), jnp.float32),
    )
    first_pos = jnp.int32(0)
    key_part = lax.all_gather(key_flat, "seq", axis=1, tiled=True)
    value_part = lax.all_gather(value_flat, "seq", axis=1, tiled=True)
    span = key_part.shape[1]
    width = 256

    def attend(state):
        for offset in range(0, span, width):
            state = fold_block(
                state,
                queries,
                key_part[:, offset : offset + width],
                value_part[:, offset : offset + width],
                first_pos + offset,
                lengths,
            )
        return state

    final_state = lax.cond(decoding, attend, lambda state: state, start_state)

    def finish(state):
        context = state[2] / state[1][..., None]
        return (
            jnp.transpose(context, (0, 2, 1, 3)).reshape(row_count, head_width).astype(jnp.bfloat16)
        )

    context_rows = lax.cond(
        decoding,
        finish,
        lambda state: jnp.zeros((row_count, head_width), jnp.bfloat16),
        final_state,
    )
    update_terms = lax.cond(
        decoding,
        lambda source: lax.dot_general(
            source, second_weight, (((1,), (1,)), ((), ())), preferred_element_type=jnp.float32
        ),
        lambda source: jnp.zeros((row_count, second_weight.shape[0]), jnp.float32),
        context_rows,
    )
    update = lax.psum_scatter(
        update_terms.astype(jnp.bfloat16), ("segment", "mp"), scatter_dimension=1, tiled=True
    ).astype(jnp.float32)
    out_width = update.shape[1]
    group_index = segment_index * lax.axis_size("mp") + lax.axis_index("mp")
    residual = lax.dynamic_slice_in_dim(dec_full, group_index * out_width, out_width, 1)
    decoder_out = (residual.astype(jnp.float32) + update).astype(jnp.bfloat16)
    return decoder_out.reshape(doc_count, pos_dev, out_width)


def solution(mesh):
    in_specs = (
        P(None, "seq", "mp"),
        P(None, "seq", "mp"),
        P("segment", None),
        P("segment", None, None, "mp"),
        P(),
    )
    out_specs = P(None, "seq", ("segment", "mp"))
    return jax.shard_map(
        on_device, mesh=mesh, in_specs=in_specs, out_specs=out_specs, check_vma=False
    )
```

profile of v0, /device:TPU:1, one launch (start us, length us, event | category | flops | bytes accessed | tf_op | source)
XLA Modules:
  0.0 470.3 jit_solution(12025478866281575327)
XLA Ops:
  6.5 0.7 all-gather.7.cloned.1.call-update
  7.3 0.0 all-gather.5.cloned.1.call-start
  7.3 0.7 all-gather.5.cloned.1.call-update
  8.0 0.0 all-gather.9.cloned.1.call-start
  8.1 11.7 %slice_bitcast_fusion = (bf16[4096,1024]{1,0:T(8,128)(2,1)}, bf16[4096,1024]{1,0:T(8,128)(2,1)}) fusion(bf16[1,2,4096,1024]{3,2,1,0:T(8,128)(2,1)} %param.18), kind=kLoop, calls=%fused_computation.292 | loop fusion | bytes 33554432 | tf_op jit(solution)/shard_map/squeeze | solution.py:58
  19.8 0.1 reduce
  19.8 31.4 %all-gather.7.cloned.1.call-done = bf16[512,4096]{1,0:T(8,128)(2,1)} async-done(((bf16[512,1024]{1,0:T(8,128)(2,1)}), bf16[512,4096]{1,0:T(8,128)(2,1)}) %all-gather.7.cloned.1.call-update) | async-done | bytes 4194320 | tf_op jit(solution)/shard_map/all_gather | solution.py:54
  51.2 17.2 %conditional.5 = (bf16[512,1024]{1,0:T(8,128)(2,1)S(1)}, bf16[512,1024]{1,0:T(8,128)(2,1)S(1)}) conditional(s32[]{:T(128)} %convert_element_type.104, (bf16[512,4096]{1,0:T(8,128)(2,1)}, bf16[4096]{0:T(1024)(128)(2,1)S(1)}, bf16[4096,1024]{1,0:T(8,128)(2,1)}, bf16[4096,1024]{1,0:T(8,128)(2,1)}) %tuple.43, () %tuple.44), branch_computations={%region_0.0_spmd, %region_2.0_spmd} | conditional | flops 8614055936 | bytes 73468000 | solution.py:77
  51.2 3.2 fusion
  54.5 9.3 %convolution_convert_fusion = bf16[512,1024]{1,0:T(8,128)(2,1)S(1)} fusion(bf16[4096,1024]{1,0:T(8,128)(2,1)} %get-tuple-element.48, bf16[512,4096]{1,0:T(8,128)(2,1)} %get-tuple-element.44, f32[4096]{0:T(1024)S(1)} %convert_element_type.71, f32[512]{0:T(512)S(1)} %add_rsqrt_fusion), kind=kOutput, calls=%fused_computation.5 | convolution fusion | flops 4303880192 | bytes 13649920 | tf_op jit(solution)/shard_map/cond/branch_0_fun/dot_general | solution.py:68
  63.8 4.6 convolution_convert_fusion.1
  68.4 1.4 collective-permute-start
  69.8 22.5 %collective-permute-done = bf16[512,1024]{1,0:T(8,128)(2,1)S(1)} collective-permute-done((bf16[512,1024]{1,0:T(8,128)(2,1)S(1)}, bf16[512,1024]{1,0:T(8,128)(2,1)S(1)}, u32[]{:S(2)}, u32[]{:S(2)}) %collective-permute-start) | collective-permute-done | bytes 1048608 | tf_op jit(solution)/shard_map/ppermute | solution.py:14
  92.3 1.0 copy-done.16
  93.3 0.0 all-gather.9.cloned.1.call-update
  93.3 0.0 all-gather.11.cloned.1.call-start
  93.4 4.2 collective-permute-start.1
  97.6 21.7 %collective-permute-done.1 = bf16[512,1024]{1,0:T(8,128)(2,1)S(1)} collective-permute-done((bf16[512,1024]{1,0:T(8,128)(2,1)S(1)}, bf16[512,1024]{1,0:T(8,128)(2,1)S(1)}, u32[]{:S(2)}, u32[]{:S(2)}) %collective-permute-start.1) | collective-permute-done | bytes 1048608 | tf_op jit(solution)/shard_map/ppermute | solution.py:14
  119.3 1.0 copy-done.17
  120.3 0.0 reduce-scatter.2.cloned.1.call-start
  120.4 0.0 all-gather.5.cloned.1.call-done
  120.4 0.1 conditional.6
  120.4 0.1 reshape.1084
  120.5 85.2 %all-gather.9.cloned.1.call-done = bf16[2,4096,1024]{2,1,0:T(8,128)(2,1)} async-done(((bf16[2,256,1024]{2,1,0:T(8,128)(2,1)}), bf16[2,4096,1024]{2,1,0:T(8,128)(2,1)}) %all-gather.9.cloned.1.call-update) | async-done | bytes 16777232 | tf_op jit(solution)/shard_map/all_gather | solution.py:96
  205.8 113.1 %all-gather.11.cloned.1.call-done = bf16[2,4096,1024]{2,1,0:T(8,128)(2,1)} async-done(((bf16[2,256,1024]{2,1,0:T(8,128)(2,1)}), bf16[2,4096,1024]{2,1,0:T(8,128)(2,1)}) %all-gather.11.cloned.1.call-update) | async-done | bytes 16777232 | tf_op jit(solution)/shard_map/all_gather | solution.py:97
  318.9 1.1 conditional.7
  318.9 1.1 broadcast_in_dim.245
  320.0 0.1 conditional.9
  320.0 0.1 broadcast.490
  320.1 1.0 copy-done.14
  321.2 141.0 %reduce-scatter.2.cloned.1.call-done = bf16[128,512]{1,0:T(8,128)(2,1)} async-done(((bf16[128,4096]{1,0:T(8,128)(2,1)}), bf16[128,512]{1,0:T(8,128)(2,1)}) %reduce-scatter.2.cloned.1.call-update) | async-done | bytes 131088 | tf_op jit(solution)/shard_map/reduce_scatter | solution.py:135
  462.1 1.7 add_convert_fusion
  (22 shorter events, 0.1 us)
Async XLA Ops:
  6.5 44.7 %all-gather.7.cloned.1.call-start = ((), (), s32[]{:S(2)}) async-start(), calls=%async_computation.2 | async-start | bytes 5242880 | tf_op jit(solution)/shard_map/all_gather | solution.py:54
  7.3 113.2 %all-gather.5.cloned.1.call-start = ((), (), s32[]{:S(2)}) async-start(), calls=%async_computation.1 | async-start | bytes 1310720 | tf_op jit(solution)/shard_map/all_gather | solution.py:55
  8.0 11.8 %copy-start.18 = (bf16[1,4096]{1,0:T(2,128)(2,1)S(1)}, bf16[1,4096]{1,0:T(2,128)(2,1)}, u32[]{:S(2)}) copy-start(bf16[1,4096]{1,0:T(2,128)(2,1)} %param.17) | copy-start | bytes 24580
  8.0 197.8 %all-gather.9.cloned.1.call-start = ((), (), s32[]{:S(2)}) async-start(), calls=%async_computation.3 | async-start | bytes 17825792 | tf_op jit(solution)/shard_map/all_gather | solution.py:96
  51.2 12.6 %slice-start = ((s8[8388608]{0:T(1024)(128)(4,1)}), s8[4194304]{0:T(1024)(128)(4,1)S(1)}, s32[]{:S(2)}) async-start(s8[8388608]{0:T(1024)(128)(4,1)} %bitcast.82), calls=%async_computation.6 | async-start | bytes 8388608 | tf_op jit(solution)/shard_map/cond
  54.4 9.4 %slice-start.1 = ((s8[8388608]{0:T(1024)(128)(4,1)}), s8[4194304]{0:T(1024)(128)(4,1)S(1)}, s32[]{:S(2)}) async-start(s8[8388608]{0:T(1024)(128)(4,1)} %bitcast.82), calls=%async_computation.7 | async-start | bytes 8388608 | tf_op jit(solution)/shard_map/cond
  54.4 9.4 %copy-start = (bf16[512,4096]{1,0:T(8,128)(2,1)S(1)}, bf16[512,4096]{1,0:T(8,128)(2,1)}, u32[]{:S(2)}) copy-start(bf16[512,4096]{1,0:T(8,128)(2,1)} %get-tuple-element.44) | copy-start | bytes 12582916 | tf_op jit(solution)/shard_map/cond
  68.4 23.9 %collective-permute-start = (bf16[512,1024]{1,0:T(8,128)(2,1)S(1)}, bf16[512,1024]{1,0:T(8,128)(2,1)S(1)}, u32[]{:S(2)}, u32[]{:S(2)}) collective-permute-start(bf16[512,1024]{1,0:T(8,128)(2,1)S(1)} %get-tuple-element.62), channel_id=1, source_target_pairs={{0,64},{1,65},{2,66},{3,67},{4,68},{5,69},{6,70},{7,71},{8,72},{9,... | collective-permute-start | bytes 3145736 | tf_op jit(solution)/shard_map/ppermute | solution.py:14
  92.3 1.0 copy-start.16
  93.3 225.5 %all-gather.11.cloned.1.call-start = ((), (), s32[]{:S(2)}) async-start(), calls=%async_computation.4 | async-start | bytes 17825792 | tf_op jit(solution)/shard_map/all_gather | solution.py:97
  93.4 25.9 %collective-permute-start.1 = (bf16[512,1024]{1,0:T(8,128)(2,1)S(1)}, bf16[512,1024]{1,0:T(8,128)(2,1)S(1)}, u32[]{:S(2)}, u32[]{:S(2)}) collective-permute-start(bf16[512,1024]{1,0:T(8,128)(2,1)S(1)} %get-tuple-element.63), channel_id=1, source_target_pairs={{0,64},{1,65},{2,66},{3,67},{4,68},{5,69},{6,70},{7,71},{8,72},{9,... | collective-permute-start | bytes 3145736 | tf_op jit(solution)/shard_map/ppermute | solution.py:14
  119.3 1.0 copy-start.17
  120.3 341.8 %reduce-scatter.2.cloned.1.call-start = ((), (), s32[]{:S(2)}) async-start(), calls=%async_computation.5 | async-start | bytes 1179648 | tf_op jit(solution)/shard_map/reduce_scatter | solution.py:135
  120.4 198.4 %copy-start.19 = (s32[2]{0:T(128)S(1)}, s32[2]{0:T(128)}, u32[]{:S(2)}) copy-start(s32[2]{0:T(128)} %param.19) | copy-start | bytes 28
  320.1 1.0 copy-start.14
Sparse Core Ops, SparseCore 0:
  9.0 42.1 all-gather.6
  52.9 20.7 all-gather.4
  93.5 112.2 all-gather.8
  207.8 111.0 all-gather.10
  321.3 140.8 reduce-scatter.1
where the time goes:
time: 472 us; the launch traced here: 470 us
  waiting for transfers between devices  416 us (88%)
  local copies, waits for them, and re-layouts  16 us (3%)
  matrix products  13.9 us (3%)
  between operations  13.2 us (3%)
  starting transfers between devices  5.72 us (1%)
  other arithmetic  4.95 us (1%)
    reduce_scatter x1, waiting for transfers between devices, on_device(): lax.psum_scatter(update_terms.astype(jnp.bfloat16), ('segment', 'mp'), sc...  141 us
    all_gather x1, waiting for transfers between devices, on_device(): value_part = lax.all_gather(value_flat, 'seq', axis=1, tiled=True)  113 us
    all_gather x1, waiting for transfers between devices, on_device(): key_part = lax.all_gather(key_flat, 'seq', axis=1, tiled=True)  85.2 us
    ppermute x2, waiting for transfers between devices, passed_along(): return lax.ppermute(shard, axis, pairs)  44.2 us
    all_gather x1, waiting for transfers between devices, on_device(): lax.all_gather(memory.reshape(mem_count, part_width), 'mp', axis=1, tiled...  31.4 us
    squeeze x1, local copies, waits for them, and re-layouts, on_device(): second_weight = weights[0, 1]  11.7 us
  transfers between devices with their start and end apart: 7, of which 6 were waited for; matrix products, arithmetic and copies ran while one was open for 6% of the time, Pallas kernels for 0%

commit v1 on v0

--- a/solution.py
+++ b/solution.py
@@ -94,7 +94,9 @@
     )
     first_pos = jnp.int32(0)
     key_part = lax.all_gather(key_flat, "seq", axis=1, tiled=True)
-    value_part = lax.all_gather(value_flat, "seq", axis=1, tiled=True)
+    value_part = jnp.concatenate(
+        lax.all_to_all(jnp.stack([value_flat] * lax.axis_size("seq")), "seq", 0, 0), axis=1
+    )
     span = key_part.shape[1]
     width = 256
 

time: 472 us -> 601 us (1.27); the launches traced: 470 us -> 591 us
  waiting for transfers between devices: 416 us -> 503 us
  local copies, waits for them, and re-layouts: 16 us -> 43.8 us
  starting transfers between devices: 5.72 us -> 12.5 us
    all_to_all x0 -> x1, waiting for transfers between devices: none -> 285 us  [on_device(): lax.all_to_all(jnp.stack([value_flat] * lax.axis_size('seq')), 'seq', 0, 0)]
    all_gather x1 -> x0, waiting for transfers between devices: 113 us -> none  [on_device(): value_part = lax.all_gather(value_flat, 'seq', axis=1, tiled=True)]
    all_gather x1, waiting for transfers between devices: 85.2 us -> 0.01 us  [on_device(): key_part = lax.all_gather(key_flat, 'seq', axis=1, tiled=True)]
    all_to_all x0 -> x1, local copies, waits for them, and re-layouts: none -> 22.4 us  [on_device(): lax.all_to_all(jnp.stack([value_flat] * lax.axis_size('seq')), 'seq', 0, 0)]
    all_to_all x0 -> x1, starting transfers between devices: none -> 6.81 us  [on_device(): lax.all_to_all(jnp.stack([value_flat] * lax.axis_size('seq')), 'seq', 0, 0)]
    another operation x2 -> x4, local copies, waits for them, and re-layouts: 0.12 us -> 6.57 us  [the longest x2 6.45 us: on_device(): jnp.stack([value_flat] * lax.axis_size('seq'))]
  transfers between devices with their start and end apart: 7 -> 7, of which waited for: 6 -> 5; matrix products, arithmetic and copies ran while one was open for 6% -> 10% of each run, Pallas kernels for 0% -> 0%
where the time goes in v1:
time: 601 us; the launch traced here: 591 us
  waiting for transfers between devices  503 us (84%)
  local copies, waits for them, and re-layouts  43.8 us (7%)
  matrix products  13.9 us (2%)
  between operations  13.2 us (2%)
  starting transfers between devices  12.5 us (2%)
    all_to_all x1, waiting for transfers between devices, on_device(): lax.all_to_all(jnp.stack([value_flat] * lax.axis_size('seq')), 'seq', 0, 0)  285 us
    reduce_scatter x1, waiting for transfers between devices, on_device(): lax.psum_scatter(update_terms.astype(jnp.bfloat16), ('segment', 'mp'), sc...  141 us
    ppermute x2, waiting for transfers between devices, passed_along(): return lax.ppermute(shard, axis, pairs)  44.2 us
    all_gather x1, waiting for transfers between devices, on_device(): lax.all_gather(memory.reshape(mem_count, part_width), 'mp', axis=1, tiled...  31.5 us
    all_to_all x1, local copies, waits for them, and re-layouts, on_device(): lax.all_to_all(jnp.stack([value_flat] * lax.axis_size('seq')), 'seq', 0, 0)  22.4 us
  transfers between devices with their start and end apart: 7, of which 5 were waited for; matrix products, arithmetic and copies ran while one was open for 10% of the time, Pallas kernels for 0%

profile of v1, /device:TPU:1, one launch (start us, length us, event | category | flops | bytes accessed | tf_op | source)
XLA Modules:
  0.0 591.2 jit_solution(1406825649999294324)
XLA Ops:
  6.5 0.7 all-gather.6.cloned.1.call-update
  7.3 0.0 all-gather.4.cloned.1.call-start
  7.3 0.7 all-gather.4.cloned.1.call-update
  8.0 0.0 all-gather.8.cloned.1.call-start
  8.1 11.6 %slice_bitcast_fusion = (bf16[4096,1024]{1,0:T(8,128)(2,1)}, bf16[4096,1024]{1,0:T(8,128)(2,1)}) fusion(bf16[1,2,4096,1024]{3,2,1,0:T(8,128)(2,1)} %param.18), kind=kLoop, calls=%fused_computation.292 | loop fusion | bytes 33554432 | tf_op jit(solution)/shard_map/squeeze | solution.py:58
  19.7 0.1 reduce
  19.7 31.5 %all-gather.6.cloned.1.call-done = bf16[512,4096]{1,0:T(8,128)(2,1)} async-done(((bf16[512,1024]{1,0:T(8,128)(2,1)}), bf16[512,4096]{1,0:T(8,128)(2,1)}) %all-gather.6.cloned.1.call-update) | async-done | bytes 4194320 | tf_op jit(solution)/shard_map/all_gather | solution.py:54
  51.2 17.2 %conditional.5 = (bf16[512,1024]{1,0:T(8,128)(2,1)S(1)}, bf16[512,1024]{1,0:T(8,128)(2,1)S(1)}) conditional(s32[]{:T(128)} %convert_element_type.104, (bf16[512,4096]{1,0:T(8,128)(2,1)}, bf16[4096]{0:T(1024)(128)(2,1)S(1)}, bf16[4096,1024]{1,0:T(8,128)(2,1)}, bf16[4096,1024]{1,0:T(8,128)(2,1)}) %tuple.43, () %tuple.44), branch_computations={%region_0.0_spmd, %region_2.0_spmd} | conditional | flops 8614055936 | bytes 73468000 | solution.py:77
  51.2 3.2 fusion
  54.5 9.3 %convolution_convert_fusion = bf16[512,1024]{1,0:T(8,128)(2,1)S(1)} fusion(bf16[4096,1024]{1,0:T(8,128)(2,1)} %get-tuple-element.48, bf16[512,4096]{1,0:T(8,128)(2,1)} %get-tuple-element.44, f32[4096]{0:T(1024)S(1)} %convert_element_type.71, f32[512]{0:T(512)S(1)} %add_rsqrt_fusion), kind=kOutput, calls=%fused_computation.5 | convolution fusion | flops 4303880192 | bytes 13649920 | tf_op jit(solution)/shard_map/cond/branch_0_fun/dot_general | solution.py:68
  63.8 4.6 convolution_convert_fusion.1
  68.4 1.4 collective-permute-start
  69.8 22.5 %collective-permute-done = bf16[512,1024]{1,0:T(8,128)(2,1)S(1)} collective-permute-done((bf16[512,1024]{1,0:T(8,128)(2,1)S(1)}, bf16[512,1024]{1,0:T(8,128)(2,1)S(1)}, u32[]{:S(2)}, u32[]{:S(2)}) %collective-permute-start) | collective-permute-done | bytes 1048608 | tf_op jit(solution)/shard_map/ppermute | solution.py:14
  92.3 1.0 copy-done.16
  93.4 4.2 collective-permute-start.1
  97.5 21.6 %collective-permute-done.1 = bf16[512,1024]{1,0:T(8,128)(2,1)S(1)} collective-permute-done((bf16[512,1024]{1,0:T(8,128)(2,1)S(1)}, bf16[512,1024]{1,0:T(8,128)(2,1)S(1)}, u32[]{:S(2)}, u32[]{:S(2)}) %collective-permute-start.1) | collective-permute-done | bytes 1048608 | tf_op jit(solution)/shard_map/ppermute | solution.py:14
  119.2 0.5 copy.18
  119.7 5.9 %stack.3 = bf16[16,2,256,1024]{2,3,1,0:T(8,128)(2,1)} broadcast(bf16[2,256,1024]{1,2,0:T(8,128)(2,1)S(1)} %copy.18), dimensions={1,2,3} | broadcast | bytes 17825792 | tf_op jit(solution)/shard_map/stack | solution.py:98
  125.6 6.8 %all-to-all-start = ((bf16[16,2,256,1024]{2,3,1,0:T(8,128)(2,1)}), bf16[16,2,256,1024]{2,3,1,0:T(8,128)(2,1)}, u32[]{:S(2)}, u32[]{:S(2)}) async-start(bf16[16,2,256,1024]{2,3,1,0:T(8,128)(2,1)} %stack.3), calls=%async_computation | async-start | bytes 33554432 | tf_op jit(solution)/shard_map/all_to_all | solution.py:98
  132.5 0.0 reduce-scatter.2.cloned.1.call-start
  132.5 0.0 all-gather.4.cloned.1.call-done
  132.5 0.1 conditional.6
  132.5 0.1 reshape.1088
  132.6 284.6 %all-to-all-done = bf16[16,2,256,1024]{2,3,1,0:T(8,128)(2,1)} async-done(((bf16[16,2,256,1024]{2,3,1,0:T(8,128)(2,1)}), bf16[16,2,256,1024]{2,3,1,0:T(8,128)(2,1)}, u32[]{:S(2)}, u32[]{:S(2)}) %all-to-all-start) | async-done | bytes 16777248 | tf_op jit(solution)/shard_map/all_to_all | solution.py:98
  417.3 22.4 %copy.19 = bf16[16,2,256,1024]{3,2,0,1:T(8,128)(2,1)} copy(bf16[16,2,256,1024]{2,3,1,0:T(8,128)(2,1)} %all-to-all-done) | data formatting | bytes 33554432 | tf_op jit(solution)/shard_map/all_to_all | solution.py:98
  439.7 1.1 conditional.7
  439.7 1.1 broadcast_in_dim.245
  440.8 0.1 conditional.9
  440.8 0.1 broadcast.491
  440.9 1.0 copy-done.14
  442.0 141.0 %reduce-scatter.2.cloned.1.call-done = bf16[128,512]{1,0:T(8,128)(2,1)} async-done(((bf16[128,4096]{1,0:T(8,128)(2,1)}), bf16[128,512]{1,0:T(8,128)(2,1)}) %reduce-scatter.2.cloned.1.call-update) | async-done | bytes 131088 | tf_op jit(solution)/shard_map/reduce_scatter | solution.py:137
  583.0 1.7 add_convert_fusion
  (22 shorter events, 0.1 us)
Async XLA Ops:
  6.5 44.7 %all-gather.6.cloned.1.call-start = ((), (), s32[]{:S(2)}) async-start(), calls=%async_computation.3 | async-start | bytes 5242880 | tf_op jit(solution)/shard_map/all_gather | solution.py:54
  7.3 125.3 %all-gather.4.cloned.1.call-start = ((), (), s32[]{:S(2)}) async-start(), calls=%async_computation.2 | async-start | bytes 1310720 | tf_op jit(solution)/shard_map/all_gather | solution.py:55
  8.0 11.7 %copy-start.17 = (bf16[1,4096]{1,0:T(2,128)(2,1)S(1)}, bf16[1,4096]{1,0:T(2,128)(2,1)}, u32[]{:S(2)}) copy-start(bf16[1,4096]{1,0:T(2,128)(2,1)} %param.17) | copy-start | bytes 24580
  8.0 431.6 %all-gather.8.cloned.1.call-start = ((), (), s32[]{:S(2)}) async-start(), calls=%async_computation.4 | async-start | bytes 17825792 | tf_op jit(solution)/shard_map/all_gather | solution.py:96
  51.2 12.6 %slice-start = ((s8[8388608]{0:T(1024)(128)(4,1)}), s8[4194304]{0:T(1024)(128)(4,1)S(1)}, s32[]{:S(2)}) async-start(s8[8388608]{0:T(1024)(128)(4,1)} %bitcast.86), calls=%async_computation.6 | async-start | bytes 8388608 | tf_op jit(solution)/shard_map/cond
  54.4 9.4 %slice-start.1 = ((s8[8388608]{0:T(1024)(128)(4,1)}), s8[4194304]{0:T(1024)(128)(4,1)S(1)}, s32[]{:S(2)}) async-start(s8[8388608]{0:T(1024)(128)(4,1)} %bitcast.86), calls=%async_computation.7 | async-start | bytes 8388608 | tf_op jit(solution)/shard_map/cond
  54.5 9.4 %copy-start = (bf16[512,4096]{1,0:T(8,128)(2,1)S(1)}, bf16[512,4096]{1,0:T(8,128)(2,1)}, u32[]{:S(2)}) copy-start(bf16[512,4096]{1,0:T(8,128)(2,1)} %get-tuple-element.44) | copy-start | bytes 12582916 | tf_op jit(solution)/shard_map/cond
  68.4 23.9 %collective-permute-start = (bf16[512,1024]{1,0:T(8,128)(2,1)S(1)}, bf16[512,1024]{1,0:T(8,128)(2,1)S(1)}, u32[]{:S(2)}, u32[]{:S(2)}) collective-permute-start(bf16[512,1024]{1,0:T(8,128)(2,1)S(1)} %get-tuple-element.62), channel_id=1, source_target_pairs={{0,64},{1,65},{2,66},{3,67},{4,68},{5,69},{6,70},{7,71},{8,72},{9,... | collective-permute-start | bytes 3145736 | tf_op jit(solution)/shard_map/ppermute | solution.py:14
  92.3 1.0 copy-start.16
  93.4 25.8 %collective-permute-start.1 = (bf16[512,1024]{1,0:T(8,128)(2,1)S(1)}, bf16[512,1024]{1,0:T(8,128)(2,1)S(1)}, u32[]{:S(2)}, u32[]{:S(2)}) collective-permute-start(bf16[512,1024]{1,0:T(8,128)(2,1)S(1)} %get-tuple-element.63), channel_id=1, source_target_pairs={{0,64},{1,65},{2,66},{3,67},{4,68},{5,69},{6,70},{7,71},{8,72},{9,... | collective-permute-start | bytes 3145736 | tf_op jit(solution)/shard_map/ppermute | solution.py:14
  125.6 291.6 %all-to-all-start = ((bf16[16,2,256,1024]{2,3,1,0:T(8,128)(2,1)}), bf16[16,2,256,1024]{2,3,1,0:T(8,128)(2,1)}, u32[]{:S(2)}, u32[]{:S(2)}) async-start(bf16[16,2,256,1024]{2,3,1,0:T(8,128)(2,1)} %stack.3), calls=%async_computation | async-start | bytes 33554432 | tf_op jit(solution)/shard_map/all_to_all | solution.py:98
  132.5 450.5 %reduce-scatter.2.cloned.1.call-start = ((), (), s32[]{:S(2)}) async-start(), calls=%async_computation.5 | async-start | bytes 1179648 | tf_op jit(solution)/shard_map/reduce_scatter | solution.py:137
  132.6 307.0 %copy-start.18 = (s32[2]{0:T(128)S(1)}, s32[2]{0:T(128)}, u32[]{:S(2)}) copy-start(s32[2]{0:T(128)} %param.19) | copy-start | bytes 28
  440.9 1.0 copy-start.14
Sparse Core Ops, SparseCore 0:
  9.0 42.1 all-gather.5
  52.9 20.7 all-gather.3
  93.5 289.3 all-gather.7
  442.1 140.8 reduce-scatter.1
